TPU v7x, 32 devices: a whole 2x2x4 slice. The times are simulated.
32 devices in a mesh: grp: 2 (over y), aux: 4 (over z), orb: 2 (over x), occ: 2 (over core).
Axes of the slice: x: 2, y: 2, z: 4, core: 2. Of those that a mesh axis runs over, the one named last changes fastest.
Arguments:
- b_tiles: bfloat16 [64, 32, 4, 128, 128], P(('grp', 'aux'), 'orb'), parts along dimension 0, may hold values from -0.25 to 0.25
- nu_block: int32 [64, 32, 4], P(('grp', 'aux'), 'orb'), parts along dimension 0, may hold values from 0 to 31
- tile_mask: int32 [64, 32, 4], P(('grp', 'aux'), 'orb'), parts along dimension 0, may hold values 0 or 1
- assignment: int32 [64], P(('grp', 'aux')), parts along dimension 0, may hold values from 0 to 31, each once
- metric_factor: float32 [64], P('grp'), parts along dimension 0, may hold values from 0.05 to 0.3
- orbitals: bfloat16 [800, 4000], P('grp'), parts along dimension 0, may hold values from -6 to 6
- occupied_index: int32 [64], P(('grp', 'occ')), parts along dimension 0, may hold values from 0 to 399
Outputs:
- exchange: float32 [8192, 4096], P(('grp', 'aux', 'occ'), 'orb'), parts along dimension 0
There are 2 independent parts, one for each index of `grp`. A program takes and returns all parts, laid end to end along the dimension named above; each array names one. Nothing has to cross between parts.
Inputs may be any that keep to these rules, and one draw needn't show every extreme that they name: `nu_block`: each entry names a column block. `assignment`: each number once. `occupied_index`: repeats may occur.
All inputs are finite; a program needn't handle non-finite values. No bound on the sum of `tile_mask` on one device may be relied on, other than what follows from the above.
Results may differ from a plain program's by a relative error of at most 0.0033.
Values may be sent and summed in bfloat16 or wider, within the bound.
A program may use at most 128 MiB of HBM per device.

v0:
```python
import jax
import jax.numpy as jnp
from jax import lax
from jax.sharding import PartitionSpec as P


def from_root(x, axis, root):
    mine = lax.axis_index(axis) == root
    return lax.psum(jnp.where(mine, x, jnp.zeros_like(x)), axis)


def per_device(b_tiles, nu_block, tile_mask, assignment, metric_factor, orbitals, occupied_index):
    naux_dev = b_tiles.shape[0]
    row_blocks = b_tiles.shape[1]
    tile_size = b_tiles.shape[3]
    n_basis = orbitals.shape[1]
    nblocks = (n_basis + tile_size - 1) // tile_size
    padded = nblocks * tile_size
    mu_dev = row_blocks * tile_size
    batch_dev = occupied_index.shape[0]
    picked = jnp.take(orbitals, occupied_index, axis=0)
    picked = jnp.pad(picked, ((0, 0), (0, padded - n_basis)))
    blocks = picked.reshape(batch_dev, nblocks, tile_size)
    chosen = blocks[:, nu_block] * tile_mask.astype(jnp.bfloat16)[None, :, :, :, None]
    half_product = jnp.einsum(
        "pmsab,ipmsb->pima", b_tiles, chosen, preferred_element_type=jnp.float32
    )
    half_product = half_product.reshape(naux_dev, batch_dev, mu_dev)
    lookup_table = (
        assignment[:, None] == jnp.arange(metric_factor.shape[0], dtype=jnp.int32)[None, :]
    ).astype(jnp.float32)
    factors = jnp.dot(lookup_table, metric_factor, precision=lax.Precision.HIGHEST)
    row_index = lax.axis_index("orb") * mu_dev + jnp.arange(mu_dev, dtype=jnp.int32)
    scaled_slab = jnp.where(
        row_index[None, None, :] < n_basis, half_product * factors[:, None, None], 0.0
    )
    half_slab = scaled_slab.astype(jnp.bfloat16).reshape(naux_dev * batch_dev, mu_dev)
    block_rows = padded // (lax.axis_size("aux") * lax.axis_size("occ"))
    everyone = lax.all_gather(half_slab, ("aux", "occ"), axis=0, tiled=True)
    group_index = lax.axis_index("aux") * lax.axis_size("occ") + lax.axis_index("occ")
    first_row = group_index * block_rows
    root_index = first_row // mu_dev
    row_offset = first_row - root_index * mu_dev
    owner_slice = lax.dynamic_slice_in_dim(everyone, row_offset, block_rows, 1)
    gathered_owner = from_root(owner_slice, "orb", root_index)
    owned_tile = lax.dot_general(
        gathered_owner, everyone, (((0,), (0,)), ((), ())), preferred_element_type=jnp.float32
    )
    return owned_tile


def solution(mesh):
    in_specs = (
        P(("grp", "aux"), "orb", None, None, None),
        P(("grp", "aux"), "orb", None),
        P(("grp", "aux"), "orb", None),
        P(("grp", "aux")),
        P("grp"),
        P("grp", None),
        P(("grp", "occ")),
    )
    out_specs = P(("grp", "aux", "occ"), "orb")
    return jax.shard_map(
        per_device, mesh=mesh, in_specs=in_specs, out_specs=out_specs, check_vma=False
    )
```

profile of v0, /device:TPU:0, one launch (start us, length us, event | category | flops | bytes accessed | tf_op | source)
XLA Modules:
  0.0 134.1 jit_solution(12434587228178125652)
XLA Ops:
  6.5 0.0 copy-start
  6.5 0.0 all-gather.2.cloned.1.call-start
  6.5 0.8 compare_and_fusion
  7.4 0.8 compare_select_fusion.1
  8.2 0.9 convolution_bitcast_fusion
  9.1 0.1 mul.38
  9.1 0.1 mul.39
  9.2 0.7 convert_element_type.10
  9.9 0.7 compare_select_fusion
  10.7 0.1 copy.12
  10.8 0.1 copy.10
  10.9 0.1 reshape.35
  11.0 0.0 copy-done
  11.1 0.6 gather_fusion
  11.7 0.1 broadcast_select_fusion
  11.8 2.7 %gather_fusion.1 = bf16[512,16,128]{2,1,0:T(8,128)(2,1)} fusion(bf16[16,32,128]{2,0,1:T(8,128)(2,1)S(1)} %copy_bitcast_fusion, s32[1024]{0:T(1024)S(1)} %pad_clamp_fusion), kind=kCustom, calls=%fused_computation.1 | custom fusion | bytes 4196352 | tf_op jit(solution)/shard_map/gather | solution.py:24
  14.5 11.9 %fusion.3 = f32[8,16,16,128]{3,1,2,0:T(8,128)} fusion(bf16[8,16,4,128,128]{4,3,2,1,0:T(8,128)(2,1)} %param.7, bf16[8,16,4,16,128]{4,3,2,1,0:T(8,128)(2,1)} %bitcast.32, bf16[8,16,4]{2,1,0:T(8,128)(2,1)S(1)} %copy.12), kind=kOutput, calls=%fused_computation.5 | convolution fusion | flops 269484032 | bytes 19923968 | tf_op jit(solution)/shard_map/pmsab,ipmsb->pima/dot_general | solution.py:25
  26.4 1.5 %copy.13 = f32[8,16,16,128]{3,2,1,0:T(8,128)S(1)} copy(f32[8,16,16,128]{3,1,2,0:T(8,128)} %fusion.3) | data formatting | bytes 2097152 | tf_op jit(solution)/shard_map/pmsab,ipmsb->pima/transpose | solution.py:25
  28.0 1.2 fusion.7
  29.2 0.0 all-gather.2.cloned.1.call-update
  29.2 0.0 all-reduce.3.cloned.1.call-start
  29.3 49.7 %all-gather.2.cloned.1.call-done = bf16[1024,2048]{1,0:T(8,128)(2,1)} async-done(((bf16[128,2048]{1,0:T(8,128)(2,1)}), bf16[1024,2048]{1,0:T(8,128)(2,1)}) %all-gather.2.cloned.1.call-update) | async-done | bytes 4194320 | tf_op jit(solution)/shard_map/all_gather | solution.py:39
  78.9 2.4 %dynamic-slice_select_fusion = bf16[1024,512]{1,0:T(8,128)(2,1)} fusion(bf16[1024,2048]{1,0:T(8,128)(2,1)} %all-gather.2.cloned.1.call-done, s32[]{:T(128)S(6)} %select_n.39, pred[]{:T(512)S(6)} %eq.16), kind=kLoop, calls=%fused_computation.11 | loop fusion | flops 524288 | bytes 2097157 | tf_op jit(solution)/shard_map/jit(_where)/select_n | solution.py:9
  81.3 0.0 all-reduce.3.cloned.1.call-update
  81.3 39.1 %all-reduce.3.cloned.1.call-done = bf16[1024,512]{1,0:T(8,128)(2,1)} async-done(((bf16[1024,512]{1,0:T(8,128)(2,1)}), bf16[1024,512]{1,0:T(8,128)(2,1)}) %all-reduce.3.cloned.1.call-update) | async-done | bytes 1048592 | tf_op jit(solution)/shard_map/psum | solution.py:9
  120.4 6.9 %fusion.11 = f32[512,2048]{1,0:T(8,128)} fusion(bf16[1024,512]{1,0:T(8,128)(2,1)} %all-reduce.3.cloned.1.call-done, bf16[1024,2048]{1,0:T(8,128)(2,1)} %all-gather.2.cloned.1.call-done), kind=kOutput, calls=%fused_computation.24 | convolution fusion | flops 2147483648 | bytes 9437184 | tf_op jit(solution)/shard_map/dot_general | solution.py:46
  (4 shorter events, 0.0 us)
Async XLA Ops:
  6.5 4.5 %copy-start = (bf16[400,4000]{1,0:T(8,128)(2,1)S(1)}, bf16[400,4000]{1,0:T(8,128)(2,1)}, u32[]{:S(2)}) copy-start(bf16[400,4000]{1,0:T(8,128)(2,1)} %param.12) | copy-start | bytes 9600004
  6.5 72.4 %all-gather.2.cloned.1.call-start = ((), (), s32[]{:S(2)}) async-start(), calls=%async_computation | async-start | bytes 4718592 | tf_op jit(solution)/shard_map/all_gather | solution.py:39
  29.2 91.2 %all-reduce.3.cloned.1.call-start = ((), (), s32[]{:S(2)}) async-start(), calls=%async_computation.1 | async-start | bytes 2097152 | tf_op jit(solution)/shard_map/psum | solution.py:9
Sparse Core Ops, SparseCore 0:
  29.3 49.5 all-gather.1
  81.4 38.8 all-reduce.2
where the time goes:
time: 134 us
  waiting for transfers between devices  88.8 us (66%)
  matrix products  19.6 us (15%)
  between operations  13.5 us (10%)
  other arithmetic  6.76 us (5%)
  local copies, waits for them, and re-layouts  5.44 us (4%)
    all_gather x1, waiting for transfers between devices, per_device(): everyone = lax.all_gather(half_slab, ('aux', 'occ'), axis=0, tiled=True)  49.7 us
    psum x1, waiting for transfers between devices, from_root(): return lax.psum(jnp.where(mine, x, jnp.zeros_like(x)), axis)  39.1 us
    dot_general x1, matrix products, per_device(): jnp.einsum('pmsab,ipmsb->pima', b_tiles, chosen, preferred_element_type=j...  11.9 us
    dot_general x1, matrix products, per_device(): lax.dot_general(gathered_owner, everyone, (((0,), (0,)), ((), ())), prefe...  6.9 us
    gather x1, local copies, waits for them, and re-layouts, per_device(): blocks[:, nu_block] * tile_mask.astype(jnp.bfloat16)[None, :, :, :, None]  2.72 us
  transfers between devices with their start and end apart: 2, of which 2 were waited for; matrix products, arithmetic and copies ran while one was open for 0% of the time, Pallas kernels for 0%

commit v1 on v0

v1 whole, which is shorter than its diff:
```python
import functools
import jax
import jax.numpy as jnp
from jax import lax
from jax.experimental import pallas as pl
from jax.experimental.pallas import tpu as pltpu
from jax.sharding import PartitionSpec as P

MESH = pl.DeviceIdType.MESH
HALVES = 2
COL_TILE = 512


def kernel(sizes, picked_ref, column_ref, assign_ref, metric_ref, b_ref, out_ref,
           chosen, stored, slabs, owner, owner_t,
           load_sem, pick_sem, line_send, line_recv, pair_send, pair_recv, orb_send, orb_recv):
    nz, nx, n_basis = sizes
    naux, row_blocks, slots, tile, _ = b_ref.shape
    nblocks, batch_dev, _ = picked_ref.shape
    block_rows, mu_dev = out_ref.shape
    np_dev = naux // 2
    per_half = np_dev // HALVES
    z, x, c = lax.axis_index("aux"), lax.axis_index("orb"), lax.axis_index("occ")
    mate = 1 - c

    def slot_of(origin, p, core):
        return (origin * np_dev + p) * 2 + core

    def root_of(core):
        first = (z * 2 + core) * block_rows
        root = first // mu_dev
        return root, pl.multiple_of(first - root * mu_dev, 128)

    my_root, my_offset = root_of(c)

    def load(p):
        return pltpu.make_async_copy(b_ref.at[c * np_dev + p], stored.at[p], load_sem.at[p])

    for p in range(np_dev):
        load(p).start()

    barrier = pltpu.get_barrier_semaphore()

    def greet(target):
        pl.semaphore_signal(barrier, inc=1, device_id=target, device_id_type=MESH)

    greet({"occ": mate})
    for step in range(1, nx):
        for core in range(2):
            greet({"orb": lax.rem(x + step, nx), "occ": core})

    @pl.when(z > 0)
    def _():
        greet({"aux": z - 1})

    @pl.when(z < nz - 1)
    def _():
        greet({"aux": z + 1})

    chosen[pl.ds(0, nblocks), pl.ds(pl.multiple_of(c * batch_dev, batch_dev), batch_dev), :] = picked_ref[...]
    chosen[nblocks] = jnp.zeros(chosen.shape[1:], chosen.dtype)
    ends = jnp.where(z > 0, 1, 0) + jnp.where(z < nz - 1, 1, 0)
    pl.semaphore_wait(barrier, 1 + 2 * (nx - 1) + ends)

    pick = pltpu.make_async_remote_copy(
        src_ref=picked_ref,
        dst_ref=chosen.at[pl.ds(0, nblocks), pl.ds(pl.multiple_of(c * batch_dev, batch_dev), batch_dev), :],
        send_sem=pick_sem.at[0], recv_sem=pick_sem.at[1],
        device_id={"occ": mate}, device_id_type=MESH)
    pick.start()
    out_ref[...] = jnp.zeros_like(out_ref)

    def line_copy(s, way):
        return pltpu.make_async_remote_copy(
            src_ref=slabs.at[s], dst_ref=slabs.at[s],
            send_sem=line_send.at[way, s], recv_sem=line_recv.at[s],
            device_id={"aux": z + (1 if way == 0 else -1)}, device_id_type=MESH)

    def pair_copy(s):
        return pltpu.make_async_remote_copy(
            src_ref=slabs.at[s], dst_ref=slabs.at[s],
            send_sem=pair_send.at[s], recv_sem=pair_recv.at[s],
            device_id={"occ": mate}, device_id_type=MESH)

    def orb_copy(s, core, step):
        _, offset = root_of(core)
        return pltpu.make_async_remote_copy(
            src_ref=slabs.at[s, :, pl.ds(offset, block_rows)], dst_ref=owner.at[s],
            send_sem=orb_send.at[core, step - 1, s], recv_sem=orb_recv.at[s],
            device_id={"orb": lax.rem(x + step, nx), "occ": core}, device_id_type=MESH)

    def spread(s):
        pair_copy(s).start()
        for core in range(2):
            @pl.when(x == root_of(core)[0])
            def _():
                for step in range(1, nx):
                    orb_copy(s, core, step).start()

    pick.wait()

    def transform(p, carry):
        load(p).wait()
        mine = c * np_dev + p
        factor = metric_ref[assign_ref[mine]]
        s = slot_of(z, p, c)

        def block(m, carry):
            base = (mine * row_blocks + m) * slots
            left = jnp.concatenate([chosen[column_ref[base + k]] for k in range(slots)], axis=1)
            right = jnp.concatenate([stored[p, m, k] for k in range(slots)], axis=1)
            product = lax.dot_general(left, right, (((1,), (1,)), ((), ())), preferred_element_type=jnp.float32)
            at = x * mu_dev + m * tile + lax.broadcasted_iota(jnp.int32, product.shape, 1)
            product = jnp.where(at < n_basis, product * factor, 0.0)
            slabs[s, :, pl.ds(pl.multiple_of(m * tile, tile), tile)] = product.astype(slabs.dtype)
            return carry

        lax.fori_loop(0, row_blocks, block, 0, unroll=4)

        @pl.when(z < nz - 1)
        def _():
            line_copy(s, 0).start()

        @pl.when(z > 0)
        def _():
            line_copy(s, 1).start()

        spread(s)
        return carry

    lax.fori_loop(0, np_dev, transform, 0)

    events = (nz - 1) * HALVES * 2

    def event(k):
        side, h, far = k % 2, (k // 2) % HALVES, k // (2 * HALVES) + 1
        return z + (2 * side - 1) * far, h, side

    def relay(k):
        origin, h, side = event(k)

        @pl.when((k < events) & (origin >= 0) & (origin < nz))
        def _():
            for q in range(per_half):
                s = slot_of(origin, h * per_half + q, c)
                line_copy(s, 0).wait_recv()

                @pl.when((side == 0) & (z < nz - 1))
                def _():
                    line_copy(s, 0).start()

                @pl.when((side == 1) & (z > 0))
                def _():
                    line_copy(s, 1).start()

                spread(s)

    rows = per_half * 2 * 2 * batch_dev
    width = min(COL_TILE, mu_dev)

    def accumulate(k):
        far_origin, far_h, _ = event(jnp.maximum(k - HALVES, 0))
        origin = jnp.where(k < HALVES, z, far_origin)
        h = jnp.where(k < HALVES, k, far_h)

        @pl.when((origin >= 0) & (origin < nz))
        def _():
            first = slot_of(origin, h * per_half, 0)
            for q in range(per_half):
                pair_copy(slot_of(origin, h * per_half + q, mate)).wait_recv()

            @pl.when(x != my_root)
            def _():
                for q in range(2 * per_half):
                    orb_copy(first + q, 0, 1).wait_recv()
                owner_t[...] = owner[pl.ds(first, 2 * per_half)].reshape(rows, block_rows).T

            @pl.when(x == my_root)
            def _():
                own = slabs[pl.ds(first, 2 * per_half), :, pl.ds(my_offset, block_rows)]
                owner_t[...] = own.reshape(rows, block_rows).T

            def columns(n, carry):
                at = pl.ds(pl.multiple_of(n * width, width), width)
                part = slabs[pl.ds(first, 2 * per_half), :, at].reshape(rows, width)
                out_ref[:, at] += jnp.dot(owner_t[...], part, preferred_element_type=jnp.float32)
                return carry

            lax.fori_loop(0, mu_dev // width, columns, 0)

    def advance(k, carry):
        relay(k)
        accumulate(k)
        return carry

    lax.fori_loop(0, events + HALVES, advance, 0)

    def drain(i, carry):
        origin = i // np_dev
        s = slot_of(origin, i % np_dev, c)
        pair_copy(s).wait_send()

        @pl.when((origin <= z) & (z < nz - 1))
        def _():
            line_copy(s, 0).wait_send()

        @pl.when((origin >= z) & (z > 0))
        def _():
            line_copy(s, 1).wait_send()

        for core in range(2):
            @pl.when(x == root_of(core)[0])
            def _():
                for step in range(1, nx):
                    orb_copy(s, core, step).wait_send()
        return carry

    lax.fori_loop(0, nz * np_dev, drain, 0)


def per_device(nz, nx, b_tiles, nu_block, tile_mask, assignment, metric_factor, orbitals, occupied_index):
    naux_dev, row_blocks, slots, tile, _ = b_tiles.shape
    n_basis = orbitals.shape[1]
    nblocks = (n_basis + tile - 1) // tile
    mu_dev = row_blocks * tile
    batch_dev = occupied_index.shape[0]
    block_rows = nblocks * tile // (nz * 2)
    picked = orbitals.at[occupied_index].get(mode="promise_in_bounds")
    picked = jnp.pad(picked, ((0, 0), (0, nblocks * tile - n_basis)))
    picked = picked.reshape(batch_dev, nblocks, tile).transpose(1, 0, 2)
    column = jnp.where(tile_mask != 0, nu_block, nblocks).reshape(-1)
    np_dev = naux_dev // 2
    nslots = nz * np_dev * 2
    batch = 2 * batch_dev
    rows = np_dev // HALVES * 2 * batch
    vmem = pl.BlockSpec(memory_space=pltpu.VMEM)
    smem = pl.BlockSpec(memory_space=pltpu.SMEM)
    return pl.pallas_call(
        functools.partial(kernel, (nz, nx, n_basis)),
        out_shape=jax.ShapeDtypeStruct((block_rows, mu_dev), jnp.float32),
        in_specs=[vmem, smem, smem, smem, pl.BlockSpec(memory_space=pl.ANY)],
        out_specs=vmem,
        scratch_shapes=[
            pltpu.VMEM((nblocks + 1, batch, tile), jnp.bfloat16),
            pltpu.VMEM((np_dev, row_blocks, slots, tile, tile), jnp.bfloat16),
            pltpu.VMEM((nslots, batch, mu_dev), jnp.bfloat16),
            pltpu.VMEM((nslots, batch, block_rows), jnp.bfloat16),
            pltpu.VMEM((block_rows, rows), jnp.bfloat16),
            pltpu.SemaphoreType.DMA((np_dev,)),
            pltpu.SemaphoreType.DMA((2,)),
            pltpu.SemaphoreType.DMA((2, nslots)),
            pltpu.SemaphoreType.DMA((nslots,)),
            pltpu.SemaphoreType.DMA((nslots,)),
            pltpu.SemaphoreType.DMA((nslots,)),
            pltpu.SemaphoreType.DMA((2, nx - 1, nslots)),
            pltpu.SemaphoreType.DMA((nslots,)),
        ],
        compiler_params=pltpu.CompilerParams(collective_id=0, has_side_effects=True),
    )(picked, column, assignment, metric_factor, b_tiles)


def solution(mesh):
    in_specs = (
        P(("grp", "aux"), "orb", None, None, None),
        P(("grp", "aux"), "orb", None),
        P(("grp", "aux"), "orb", None),
        P(("grp", "aux")),
        P("grp"),
        P("grp", None),
        P(("grp", "occ")),
    )
    out_specs = P(("grp", "aux", "occ"), "orb")
    body = functools.partial(per_device, mesh.shape["aux"], mesh.shape["orb"])
    return jax.shard_map(body, mesh=mesh, in_specs=in_specs, out_specs=out_specs, check_vma=False)
```

time: 134 us -> 58.8 us (0.44)
  waiting for transfers between devices: 88.8 us -> 0 us
  Pallas kernels: 0 us -> 49.9 us
  matrix products: 19.6 us -> 0 us
  between operations: 13.5 us -> 0.02 us
  other arithmetic: 6.76 us -> 1.73 us
  local copies, waits for them, and re-layouts: 5.44 us -> 6.82 us
    pallas_call x0 -> x1, Pallas kernels: none -> 49.9 us  [per_device(): pl.pallas_call(functools.partial(kernel, (nz, nx, n_basis)), out_shape=ja...]
    all_gather x1 -> x0, waiting for transfers between devices: 49.7 us -> none  [per_device(): everyone = lax.all_gather(half_slab, ('aux', 'occ'), axis=0, tiled=True)]
    psum x1 -> x0, waiting for transfers between devices: 39.1 us -> none  [from_root(): return lax.psum(jnp.where(mine, x, jnp.zeros_like(x)), axis)]
    dot_general x3 -> x0, matrix products: 19.6 us -> none  [the longest x1 11.9 us: per_device(): jnp.einsum('pmsab,ipmsb->pima', b_tiles, chosen, preferred_element_type=j...]
    unnamed x2 -> x3, local copies, waits for them, and re-layouts: 0.01 us -> 4.7 us
    gather x2 -> x1, local copies, waits for them, and re-layouts: 3.35 us -> 0.62 us  [per_device(): picked = orbitals.at[occupied_index].get(mode='promise_in_bounds')]
    select_n x4 -> x2, other arithmetic: 4 us -> 1.72 us  [the longest x1 0.92 us: per_device(): column = jnp.where(tile_mask != 0, nu_block, nblocks).reshape(-1)]
    convert_element_type x2 -> x0, other arithmetic: 1.92 us -> none  [the longest x1 1.19 us: per_device(): scaled_slab.astype(jnp.bfloat16).reshape(naux_dev * batch_dev, mu_dev)]
  transfers between devices with their start and end apart: 2 -> 0, of which waited for: 2 -> 0; matrix products, arithmetic and copies ran while one was open for 0% -> 0% of each run, Pallas kernels for 0% -> 0%
where the time goes in v1:
time: 58.8 us; the launch traced here: 58.5 us
  Pallas kernels  49.9 us (85%)
  local copies, waits for them, and re-layouts  6.82 us (12%)
  other arithmetic  1.73 us (3%)
    pallas_call x1, Pallas kernels, per_device(): pl.pallas_call(functools.partial(kernel, (nz, nx, n_basis)), out_shape=ja...  49.9 us
    unnamed x3, local copies, waits for them, and re-layouts  4.7 us

profile of v1, /device:TPU:0, one launch (start us, length us, event | category | flops | bytes accessed | tf_op | source)
XLA Modules:
  0.0 58.5 jit_solution(8873982985264013852)
XLA Ops:
  0.0 0.0 copy-start
  0.0 0.8 %compare_select_fusion.1 = s32[16]{0:T(128)S(1)} fusion(s32[16]{0:T(128)} %param.13), kind=kLoop, calls=%fused_computation.5 | loop fusion | flops 48 | bytes 128 | tf_op jit(solution)/shard_map/select_n | solution.py:228
  0.8 0.9 %compare_select_fusion = s32[8,16,4]{1,2,0:T(4,128)S(1)} fusion(s32[8,16,4]{1,2,0:T(4,128)} %param.8, s32[8,16,4]{1,2,0:T(4,128)} %param.9), kind=kLoop, calls=%fused_computation.3 | loop fusion | flops 1024 | bytes 6144 | tf_op jit(solution)/shard_map/jit(_where)/select_n | solution.py:231
  1.7 0.1 copy.9
  1.9 0.7 %reshape.7.column_ref = s32[512]{0:T(512)} reshape(s32[8,16,4]{2,1,0:T(8,128)S(1)} %copy.9) | data formatting | bytes 4096 | tf_op jit(solution)/shard_map/reshape | solution.py:231
  2.5 0.0 copy-done
  2.5 0.6 %gather_fusion = bf16[16,4000]{1,0:T(8,128)(2,1)S(1)} fusion(bf16[400,4000]{1,0:T(8,128)(2,1)S(1)} %copy-done, s32[1024]{0:T(1024)S(1)} %pad_clamp_fusion), kind=kCustom, calls=%fused_computation | custom fusion | bytes 256064 | tf_op jit(solution)/shard_map/gather | solution.py:228
  3.2 0.7 %bitcast_bitcast_fusion.picked_ref = bf16[32,16,128]{2,1,0:T(8,128)(2,1)} fusion(bf16[16,4000]{1,0:T(8,128)(2,1)S(1)} %gather_fusion), kind=kLoop, calls=%fused_computation.1 | loop fusion | bytes 259072 | tf_op jit(solution)/shard_map/transpose | solution.py:230
  3.9 49.9 %shard_map.73 = f32[512,2048]{1,0:T(8,128)} custom-call(bf16[32,16,128]{2,1,0:T(8,128)(2,1)} %bitcast_bitcast_fusion.picked_ref, s32[512]{0:T(512)} %reshape.7.column_ref, s32[8]{0:T(128)} %assign_ref.1, f32[32]{0:T(128)} %metric_ref.1, bf16[8,16,4,128,128]{4,3,2,1,0:T(8,128)(2,1)} %b_ref.1), custom_call_target="tpu_custom_call" | custom-call | tf_op jit(solution)/shard_map/pallas_call | solution.py:238
  53.8 4.7 %copy.13 = f32[512,2048]{1,0:T(8,128)} copy(f32[512,2048]{1,0:T(8,128)} %shard_map.73) | data formatting | bytes 8388608
  (1 shorter events, 0.0 us)
Async XLA Ops:
  0.0 2.5 %copy-start = (bf16[400,4000]{1,0:T(8,128)(2,1)S(1)}, bf16[400,4000]{1,0:T(8,128)(2,1)}, u32[]{:S(2)}) copy-start(bf16[400,4000]{1,0:T(8,128)(2,1)} %param.12) | copy-start | bytes 9600004

commit v2 on v1

--- a/solution.py
+++ b/solution.py
@@ -9,9 +9,10 @@
 MESH = pl.DeviceIdType.MESH
 HALVES = 2
 COL_TILE = 512
-
-
-def kernel(sizes, picked_ref, column_ref, assign_ref, metric_ref, b_ref, out_ref,
+VMEM_GRANT = 44 << 20
+
+
+def kernel(sizes, picked_ref, column_ref, mask_ref, assign_ref, metric_ref, b_ref, out_ref,
            chosen, stored, slabs, owner, owner_t,
            load_sem, pick_sem, line_send, line_recv, pair_send, pair_recv, orb_send, orb_recv):
     nz, nx, n_basis = sizes
@@ -106,8 +107,11 @@
         s = slot_of(z, p, c)
 
         def block(m, carry):
-            base = (mine * row_blocks + m) * slots
-            left = jnp.concatenate([chosen[column_ref[base + k]] for k in range(slots)], axis=1)
+            def pick_block(k):
+                kept = mask_ref[mine, k, m]
+                return chosen[kept * column_ref[mine, k, m] + (1 - kept) * nblocks]
+
+            left = jnp.concatenate([pick_block(k) for k in range(slots)], axis=1)
             right = jnp.concatenate([stored[p, m, k] for k in range(slots)], axis=1)
             product = lax.dot_general(left, right, (((1,), (1,)), ((), ())), preferred_element_type=jnp.float32)
             at = x * mu_dev + m * tile + lax.broadcasted_iota(jnp.int32, product.shape, 1)
@@ -225,10 +229,9 @@
     mu_dev = row_blocks * tile
     batch_dev = occupied_index.shape[0]
     block_rows = nblocks * tile // (nz * 2)
-    picked = orbitals.at[occupied_index].get(mode="promise_in_bounds")
+    picked = orbitals.at[occupied_index].get(mode="promise_in_bounds", wrap_negative_indices=False)
     picked = jnp.pad(picked, ((0, 0), (0, nblocks * tile - n_basis)))
     picked = picked.reshape(batch_dev, nblocks, tile).transpose(1, 0, 2)
-    column = jnp.where(tile_mask != 0, nu_block, nblocks).reshape(-1)
     np_dev = naux_dev // 2
     nslots = nz * np_dev * 2
     batch = 2 * batch_dev
@@ -238,7 +241,7 @@
     return pl.pallas_call(
         functools.partial(kernel, (nz, nx, n_basis)),
         out_shape=jax.ShapeDtypeStruct((block_rows, mu_dev), jnp.float32),
-        in_specs=[vmem, smem, smem, smem, pl.BlockSpec(memory_space=pl.ANY)],
+        in_specs=[vmem, smem, smem, smem, smem, pl.BlockSpec(memory_space=pltpu.HBM)],
         out_specs=vmem,
         scratch_shapes=[
             pltpu.VMEM((nblocks + 1, batch, tile), jnp.bfloat16),
@@ -255,8 +258,10 @@
             pltpu.SemaphoreType.DMA((2, nx - 1, nslots)),
             pltpu.SemaphoreType.DMA((nslots,)),
         ],
-        compiler_params=pltpu.CompilerParams(collective_id=0, has_side_effects=True),
-    )(picked, column, assignment, metric_factor, b_tiles)
+        compiler_params=pltpu.CompilerParams(
+            collective_id=0, has_side_effects=True,
+            vmem_limit_bytes=VMEM_GRANT),
+    )(picked, nu_block.transpose(0, 2, 1), tile_mask.transpose(0, 2, 1), assignment, metric_factor, b_tiles)
 
 
 def solution(mesh):

time: 58.8 us -> 55.8 us (0.949)
  Pallas kernels: 49.9 us -> 48.1 us
  other arithmetic: 1.73 us -> 0.81 us
    pallas_call x1, Pallas kernels: 49.9 us -> 48.1 us  [per_device(): pl.pallas_call(functools.partial(kernel, (nz, nx, n_basis)), out_shape=ja...]
    select_n x2 -> x0, other arithmetic: 1.72 us -> none  [the longest x1 0.92 us: per_device(): column = jnp.where(tile_mask != 0, nu_block, nblocks).reshape(-1)]
    unnamed x3 -> x11, local copies, waits for them, and re-layouts: 4.7 us -> 5.89 us
    gather x1, other arithmetic: 0.01 us -> 0.81 us  [per_device(): orbitals.at[occupied_index]]
    reshape x1 -> x0, local copies, waits for them, and re-layouts: 0.68 us -> none  [per_device(): column = jnp.where(tile_mask != 0, nu_block, nblocks).reshape(-1)]
    transpose x1, local copies, waits for them, and re-layouts: 0.68 us -> 0.03 us  [per_device(): picked = picked.reshape(batch_dev, nblocks, tile).transpose(1, 0, 2)]
where the time goes in v2:
time: 55.8 us; the launch traced here: 55.5 us
  Pallas kernels  48.1 us (86%)
  local copies, waits for them, and re-layouts  6.54 us (12%)
  other arithmetic  0.81 us (1%)
    pallas_call x1, Pallas kernels, per_device(): pl.pallas_call(functools.partial(kernel, (nz, nx, n_basis)), out_shape=ja...  48.1 us
    unnamed x11, local copies, waits for them, and re-layouts  5.89 us

profile of v2, /device:TPU:0, one launch (start us, length us, event | category | flops | bytes accessed | tf_op | source)
XLA Modules:
  0.0 55.5 jit_solution(13780672356967592353)
XLA Ops:
  0.0 0.0 copy-start
  0.0 0.8 %pad_clamp_fusion = s32[1024]{0:T(1024)S(1)} fusion(s32[16]{0:T(128)} %param.13), kind=kLoop, calls=%fused_computation.3 | loop fusion | flops 1024 | bytes 4160 | tf_op jit(solution)/shard_map/gather | solution.py:232
  0.8 1.1 %copy-done = bf16[400,4000]{1,0:T(8,128)(2,1)S(1)} copy-done((bf16[400,4000]{1,0:T(8,128)(2,1)S(1)}, bf16[400,4000]{1,0:T(8,128)(2,1)}, u32[]{:S(2)}) %copy-start) | copy-done | bytes 3200024
  1.9 0.6 %gather_fusion = bf16[16,4000]{1,0:T(8,128)(2,1)S(1)} fusion(bf16[400,4000]{1,0:T(8,128)(2,1)S(1)} %copy-done, s32[1024]{0:T(1024)S(1)} %pad_clamp_fusion), kind=kCustom, calls=%fused_computation | custom fusion | bytes 256064 | tf_op jit(solution)/shard_map/gather | solution.py:232
  2.6 0.0 copy-start.1
  2.6 0.7 %copy-done.1 = s32[8,16,4]{1,2,0:T(4,128)S(1)} copy-done((s32[8,16,4]{1,2,0:T(4,128)S(1)}, s32[8,16,4]{1,2,0:T(4,128)}, u32[]{:S(2)}) %copy-start.1) | copy-done | bytes 2072
  3.3 0.0 copy-start.2
  3.3 0.7 %copy-done.2 = s32[8,16,4]{1,2,0:T(4,128)S(1)} copy-done((s32[8,16,4]{1,2,0:T(4,128)S(1)}, s32[8,16,4]{1,2,0:T(4,128)}, u32[]{:S(2)}) %copy-start.2) | copy-done | bytes 2072
  4.0 0.0 copy-start.3
  4.0 0.7 %copy-done.3 = s32[8]{0:T(128)S(1)} copy-done((s32[8]{0:T(128)S(1)}, s32[8]{0:T(128)}, u32[]{:S(2)}) %copy-start.3) | copy-done | bytes 56
  4.7 0.0 copy-start.4
  4.7 0.7 %copy-done.4 = f32[32]{0:T(128)S(1)} copy-done((f32[32]{0:T(128)S(1)}, f32[32]{0:T(128)}, u32[]{:S(2)}) %copy-start.4) | copy-done | bytes 152
  5.4 48.1 %shard_map.73 = f32[512,2048]{1,0:T(8,128)S(1)} custom-call(bf16[32,16,128]{2,1,0:T(8,128)(2,1)S(1)} %bitcast_bitcast_fusion.picked_ref, s32[8,4,16]{2,1,0:T(4,128)S(1)} %bitcast.9, s32[8,4,16]{2,1,0:T(4,128)S(1)} %bitcast.10, s32[8]{0:T(128)S(1)} %copy-done.3, f32[32]{0:T(128)S(1)} %copy-done.4, bf16[8,16,4,128,128]{4,3,2,1,0:T(8,128)(2,1)} %b_ref.1), custom_call_target="tpu_custom_call" | custom-call | tf_op jit(solution)/shard_map/pallas_call | solution.py:241
  53.5 2.0 %copy.12 = f32[512,2048]{1,0:T(8,128)} copy(f32[512,2048]{1,0:T(8,128)S(1)} %shard_map.73) | data formatting | bytes 8388608
  (1 shorter events, 0.0 us)
Async XLA Ops:
  0.0 1.9 %copy-start = (bf16[400,4000]{1,0:T(8,128)(2,1)S(1)}, bf16[400,4000]{1,0:T(8,128)(2,1)}, u32[]{:S(2)}) copy-start(bf16[400,4000]{1,0:T(8,128)(2,1)} %param.12) | copy-start | bytes 9600004
  2.6 0.7 %copy-start.1 = (s32[8,16,4]{1,2,0:T(4,128)S(1)}, s32[8,16,4]{1,2,0:T(4,128)}, u32[]{:S(2)}) copy-start(s32[8,16,4]{1,2,0:T(4,128)} %param.8) | copy-start | bytes 6148
  3.3 0.7 %copy-start.2 = (s32[8,16,4]{1,2,0:T(4,128)S(1)}, s32[8,16,4]{1,2,0:T(4,128)}, u32[]{:S(2)}) copy-start(s32[8,16,4]{1,2,0:T(4,128)} %param.9) | copy-start | bytes 6148
  4.0 0.7 %copy-start.3 = (s32[8]{0:T(128)S(1)}, s32[8]{0:T(128)}, u32[]{:S(2)}) copy-start(s32[8]{0:T(128)} %assign_ref.1) | copy-start | bytes 100
  4.7 0.7 %copy-start.4 = (f32[32]{0:T(128)S(1)}, f32[32]{0:T(128)}, u32[]{:S(2)}) copy-start(f32[32]{0:T(128)} %metric_ref.1) | copy-start | bytes 388

commit v3 on v2

--- a/solution.py
+++ b/solution.py
@@ -236,6 +236,8 @@
     nslots = nz * np_dev * 2
     batch = 2 * batch_dev
     rows = np_dev // HALVES * 2 * batch
+    tables = [nu_block.transpose(0, 2, 1), tile_mask.transpose(0, 2, 1), assignment, metric_factor]
+    tables = [pltpu.with_memory_space_constraint(table, pltpu.HBM) for table in tables]
     vmem = pl.BlockSpec(memory_space=pltpu.VMEM)
     smem = pl.BlockSpec(memory_space=pltpu.SMEM)
     return pl.pallas_call(
@@ -261,7 +263,7 @@
         compiler_params=pltpu.CompilerParams(
             collective_id=0, has_side_effects=True,
             vmem_limit_bytes=VMEM_GRANT),
-    )(picked, nu_block.transpose(0, 2, 1), tile_mask.transpose(0, 2, 1), assignment, metric_factor, b_tiles)
+    )(picked, *tables, b_tiles)
 
 
 def solution(mesh):

time: 55.8 us -> 53.1 us (0.952)
  local copies, waits for them, and re-layouts: 6.54 us -> 3.8 us
    unnamed x11 -> x3, local copies, waits for them, and re-layouts: 5.89 us -> 3.15 us
where the time goes in v3:
time: 53.1 us; the launch traced here: 52.9 us
  Pallas kernels  48.3 us (91%)
  local copies, waits for them, and re-layouts  3.8 us (7%)
  other arithmetic  0.81 us (2%)
    pallas_call x1, Pallas kernels, per_device(): pl.pallas_call(functools.partial(kernel, (nz, nx, n_basis)), out_shape=ja...  48.3 us
    unnamed x3, local copies, waits for them, and re-layouts  3.15 us

profile of v3, /device:TPU:0, one launch (start us, length us, event | category | flops | bytes accessed | tf_op | source)
XLA Modules:
  0.0 52.9 jit_solution(871604013426621390)
XLA Ops:
  0.0 0.0 copy-start
  0.0 0.8 %pad_clamp_fusion = s32[1024]{0:T(1024)S(1)} fusion(s32[16]{0:T(128)} %param.13), kind=kLoop, calls=%fused_computation.3 | loop fusion | flops 1024 | bytes 4160 | tf_op jit(solution)/shard_map/gather | solution.py:232
  0.8 1.1 %copy-done = bf16[400,4000]{1,0:T(8,128)(2,1)S(1)} copy-done((bf16[400,4000]{1,0:T(8,128)(2,1)S(1)}, bf16[400,4000]{1,0:T(8,128)(2,1)}, u32[]{:S(2)}) %copy-start) | copy-done | bytes 3200024
  1.9 0.6 %gather_fusion = bf16[16,4000]{1,0:T(8,128)(2,1)S(1)} fusion(bf16[400,4000]{1,0:T(8,128)(2,1)S(1)} %copy-done, s32[1024]{0:T(1024)S(1)} %pad_clamp_fusion), kind=kCustom, calls=%fused_computation | custom fusion | bytes 256064 | tf_op jit(solution)/shard_map/gather | solution.py:232
  2.6 48.3 %shard_map.73 = f32[512,2048]{1,0:T(8,128)S(1)} custom-call(bf16[32,16,128]{2,1,0:T(8,128)(2,1)S(1)} %bitcast_bitcast_fusion.picked_ref, s32[8,4,16]{2,1,0:T(4,128)} %bitcast.9, s32[8,4,16]{2,1,0:T(4,128)} %bitcast.10, s32[8]{0:T(128)} %assign_ref.1, f32[32]{0:T(128)} %metric_ref.1, bf16[8,16,4,128,128]{4,3,2,1,0:T(8,128)(2,1)} %b_ref.1), custom_call_target="tpu_custom_call" | custom-call | tf_op jit(solution)/shard_map/pallas_call | solution.py:243
  50.9 2.0 %copy.12 = f32[512,2048]{1,0:T(8,128)} copy(f32[512,2048]{1,0:T(8,128)S(1)} %shard_map.73) | data formatting | bytes 8388608
  (1 shorter events, 0.0 us)
Async XLA Ops:
  0.0 1.9 %copy-start = (bf16[400,4000]{1,0:T(8,128)(2,1)S(1)}, bf16[400,4000]{1,0:T(8,128)(2,1)}, u32[]{:S(2)}) copy-start(bf16[400,4000]{1,0:T(8,128)(2,1)} %param.12) | copy-start | bytes 9600004

commit v4 on v3

--- a/solution.py
+++ b/solution.py
@@ -9,23 +9,25 @@
 MESH = pl.DeviceIdType.MESH
 HALVES = 2
 COL_TILE = 512
+PIECES = 2
 VMEM_GRANT = 44 << 20
 
 
-def kernel(sizes, picked_ref, column_ref, mask_ref, assign_ref, metric_ref, b_ref, out_ref,
-           chosen, stored, slabs, owner, owner_t,
-           load_sem, pick_sem, line_send, line_recv, pair_send, pair_recv, orb_send, orb_recv):
+def kernel(sizes, picked_ref, column_hbm, mask_hbm, assign_hbm, metric_hbm, b_ref, out_ref,
+           column_ref, mask_ref, assign_ref, metric_ref, total, chosen, stored, slabs, owner, owner_t,
+           table_sem, out_sem, load_sem, pick_sem, line_send, line_recv, pair_send, pair_recv, orb_send, orb_recv):
     nz, nx, n_basis = sizes
     naux, row_blocks, slots, tile, _ = b_ref.shape
     nblocks, batch_dev, _ = picked_ref.shape
     block_rows, mu_dev = out_ref.shape
     np_dev = naux // 2
+    piece = 2 * batch_dev // PIECES
     per_half = np_dev // HALVES
     z, x, c = lax.axis_index("aux"), lax.axis_index("orb"), lax.axis_index("occ")
     mate = 1 - c
 
     def slot_of(origin, p, core):
-        return (origin * np_dev + p) * 2 + core
+        return ((origin * np_dev + p) * 2 + core) * PIECES
 
     def root_of(core):
         first = (z * 2 + core) * block_rows
@@ -37,7 +39,15 @@
     def load(p):
         return pltpu.make_async_copy(b_ref.at[c * np_dev + p], stored.at[p], load_sem.at[p])
 
-    for p in range(np_dev):
+    load(0).start()
+    tables = [
+        pltpu.make_async_copy(source, target, table_sem.at[n])
+        for n, (source, target) in enumerate((
+            (column_hbm, column_ref), (mask_hbm, mask_ref), (assign_hbm, assign_ref), (metric_hbm, metric_ref)))
+    ]
+    for table in tables:
+        table.start()
+    for p in range(1, np_dev):
         load(p).start()
 
     barrier = pltpu.get_barrier_semaphore()
@@ -69,7 +79,8 @@
         send_sem=pick_sem.at[0], recv_sem=pick_sem.at[1],
         device_id={"occ": mate}, device_id_type=MESH)
     pick.start()
-    out_ref[...] = jnp.zeros_like(out_ref)
+    for table in tables:
+        table.wait()
 
     def line_copy(s, way):
         return pltpu.make_async_remote_copy(
@@ -116,24 +127,28 @@
             product = lax.dot_general(left, right, (((1,), (1,)), ((), ())), preferred_element_type=jnp.float32)
             at = x * mu_dev + m * tile + lax.broadcasted_iota(jnp.int32, product.shape, 1)
             product = jnp.where(at < n_basis, product * factor, 0.0)
-            slabs[s, :, pl.ds(pl.multiple_of(m * tile, tile), tile)] = product.astype(slabs.dtype)
+            for g in range(PIECES):
+                part = product[g * piece:(g + 1) * piece]
+                slabs[s + g, :, pl.ds(pl.multiple_of(m * tile, tile), tile)] = part.astype(slabs.dtype)
             return carry
 
         lax.fori_loop(0, row_blocks, block, 0, unroll=4)
 
-        @pl.when(z < nz - 1)
-        def _():
-            line_copy(s, 0).start()
-
-        @pl.when(z > 0)
-        def _():
-            line_copy(s, 1).start()
-
-        spread(s)
+        for g in range(PIECES):
+            @pl.when(z < nz - 1)
+            def _():
+                line_copy(s + g, 0).start()
+
+            @pl.when(z > 0)
+            def _():
+                line_copy(s + g, 1).start()
+
+            spread(s + g)
         return carry
 
     lax.fori_loop(0, np_dev, transform, 0)
 
+    total[...] = jnp.zeros_like(total)
     events = (nz - 1) * HALVES * 2
 
     def event(k):
@@ -145,8 +160,8 @@
 
         @pl.when((k < events) & (origin >= 0) & (origin < nz))
         def _():
-            for q in range(per_half):
-                s = slot_of(origin, h * per_half + q, c)
+            for q in range(per_half * PIECES):
+                s = slot_of(origin, h * per_half + q // PIECES, c) + q % PIECES
                 line_copy(s, 0).wait_recv()
 
                 @pl.when((side == 0) & (z < nz - 1))
@@ -159,8 +174,17 @@
 
                 spread(s)
 
-    rows = per_half * 2 * 2 * batch_dev
+    count = per_half * 2 * PIECES
+    rows = count * piece
     width = min(COL_TILE, mu_dev)
+
+    before, after = z, nz - 1 - z
+    last_side = jnp.where(after >= before, 1, 0)
+    last = HALVES + jnp.maximum(before, after) * HALVES * 2 - 2 + last_side
+
+    def out_copy(n):
+        at = pl.ds(pl.multiple_of(n * width, width), width)
+        return pltpu.make_async_copy(total.at[:, at], out_ref.at[:, at], out_sem.at[n])
 
     def accumulate(k):
         far_origin, far_h, _ = event(jnp.maximum(k - HALVES, 0))
@@ -170,24 +194,28 @@
         @pl.when((origin >= 0) & (origin < nz))
         def _():
             first = slot_of(origin, h * per_half, 0)
-            for q in range(per_half):
-                pair_copy(slot_of(origin, h * per_half + q, mate)).wait_recv()
+            for q in range(per_half * PIECES):
+                pair_copy(slot_of(origin, h * per_half + q // PIECES, mate) + q % PIECES).wait_recv()
 
             @pl.when(x != my_root)
             def _():
-                for q in range(2 * per_half):
+                for q in range(count):
                     orb_copy(first + q, 0, 1).wait_recv()
-                owner_t[...] = owner[pl.ds(first, 2 * per_half)].reshape(rows, block_rows).T
+                owner_t[...] = owner[pl.ds(first, count)].reshape(rows, block_rows).T
 
             @pl.when(x == my_root)
             def _():
-                own = slabs[pl.ds(first, 2 * per_half), :, pl.ds(my_offset, block_rows)]
+                own = slabs[pl.ds(first, count), :, pl.ds(my_offset, block_rows)]
                 owner_t[...] = own.reshape(rows, block_rows).T
 
             def columns(n, carry):
                 at = pl.ds(pl.multiple_of(n * width, width), width)
-                part = slabs[pl.ds(first, 2 * per_half), :, at].reshape(rows, width)
-                out_ref[:, at] += jnp.dot(owner_t[...], part, preferred_element_type=jnp.float32)
+                part = slabs[pl.ds(first, count), :, at].reshape(rows, width)
+                total[:, at] += jnp.dot(owner_t[...], part, preferred_element_type=jnp.float32)
+
+                @pl.when(k == last)
+                def _():
+                    out_copy(n).start()
                 return carry
 
             lax.fori_loop(0, mu_dev // width, columns, 0)
@@ -200,8 +228,9 @@
     lax.fori_loop(0, events + HALVES, advance, 0)
 
     def drain(i, carry):
-        origin = i // np_dev
-        s = slot_of(origin, i % np_dev, c)
+        origin = i // (np_dev * PIECES)
+        left = i % (np_dev * PIECES)
+        s = slot_of(origin, left // PIECES, c) + left % PIECES
         pair_copy(s).wait_send()
 
         @pl.when((origin <= z) & (z < nz - 1))
@@ -219,7 +248,9 @@
                     orb_copy(s, core, step).wait_send()
         return carry
 
-    lax.fori_loop(0, nz * np_dev, drain, 0)
+    lax.fori_loop(0, nz * np_dev * PIECES, drain, 0)
+    for n in range(mu_dev // width):
+        out_copy(n).wait()
 
 
 def per_device(nz, nx, b_tiles, nu_block, tile_mask, assignment, metric_factor, orbitals, occupied_index):
@@ -233,24 +264,27 @@
     picked = jnp.pad(picked, ((0, 0), (0, nblocks * tile - n_basis)))
     picked = picked.reshape(batch_dev, nblocks, tile).transpose(1, 0, 2)
     np_dev = naux_dev // 2
-    nslots = nz * np_dev * 2
+    nslots = nz * np_dev * 2 * PIECES
+    piece = 2 * batch_dev // PIECES
     batch = 2 * batch_dev
     rows = np_dev // HALVES * 2 * batch
     tables = [nu_block.transpose(0, 2, 1), tile_mask.transpose(0, 2, 1), assignment, metric_factor]
     tables = [pltpu.with_memory_space_constraint(table, pltpu.HBM) for table in tables]
     vmem = pl.BlockSpec(memory_space=pltpu.VMEM)
-    smem = pl.BlockSpec(memory_space=pltpu.SMEM)
     return pl.pallas_call(
         functools.partial(kernel, (nz, nx, n_basis)),
         out_shape=jax.ShapeDtypeStruct((block_rows, mu_dev), jnp.float32),
-        in_specs=[vmem, smem, smem, smem, smem, pl.BlockSpec(memory_space=pltpu.HBM)],
-        out_specs=vmem,
-        scratch_shapes=[
+        in_specs=[vmem] + [pl.BlockSpec(memory_space=pltpu.HBM)] * 5,
+        out_specs=pl.BlockSpec(memory_space=pl.ANY),
+        scratch_shapes=[pltpu.SMEM(table.shape, table.dtype) for table in tables] + [
+            pltpu.VMEM((block_rows, mu_dev), jnp.float32),
             pltpu.VMEM((nblocks + 1, batch, tile), jnp.bfloat16),
             pltpu.VMEM((np_dev, row_blocks, slots, tile, tile), jnp.bfloat16),
-            pltpu.VMEM((nslots, batch, mu_dev), jnp.bfloat16),
-            pltpu.VMEM((nslots, batch, block_rows), jnp.bfloat16),
+            pltpu.VMEM((nslots, piece, mu_dev), jnp.bfloat16),
+            pltpu.VMEM((nslots, piece, block_rows), jnp.bfloat16),
             pltpu.VMEM((block_rows, rows), jnp.bfloat16),
+            pltpu.SemaphoreType.DMA((len(tables),)),
+            pltpu.SemaphoreType.DMA((mu_dev // min(COL_TILE, mu_dev),)),
             pltpu.SemaphoreType.DMA((np_dev,)),
             pltpu.SemaphoreType.DMA((2,)),
             pltpu.SemaphoreType.DMA((2, nslots)),

time: 53.1 us -> 55.8 us (1.051)
  Pallas kernels: 48.3 us -> 51 us
    pallas_call x1, Pallas kernels: 48.3 us -> 51 us  [per_device(): pl.pallas_call(functools.partial(kernel, (nz, nx, n_basis)), out_shape=ja...]
where the time goes in v4:
time: 55.8 us; the launch traced here: 55.6 us
  Pallas kernels  51 us (91%)
  local copies, waits for them, and re-layouts  3.8 us (7%)
  other arithmetic  0.81 us (1%)
    pallas_call x1, Pallas kernels, per_device(): pl.pallas_call(functools.partial(kernel, (nz, nx, n_basis)), out_shape=ja...  51 us
    unnamed x3, local copies, waits for them, and re-layouts  3.15 us

profile of v4, /device:TPU:0, one launch (start us, length us, event | category | flops | bytes accessed | tf_op | source)
XLA Modules:
  0.0 55.6 jit_solution(15244784596957166149)
XLA Ops:
  0.0 0.0 copy-start
  0.0 0.8 %pad_clamp_fusion = s32[1024]{0:T(1024)S(1)} fusion(s32[16]{0:T(128)} %param.13), kind=kLoop, calls=%fused_computation.3 | loop fusion | flops 1024 | bytes 4160 | tf_op jit(solution)/shard_map/gather | solution.py:263
  0.8 1.1 %copy-done = bf16[400,4000]{1,0:T(8,128)(2,1)S(1)} copy-done((bf16[400,4000]{1,0:T(8,128)(2,1)S(1)}, bf16[400,4000]{1,0:T(8,128)(2,1)}, u32[]{:S(2)}) %copy-start) | copy-done | bytes 3200024
  1.9 0.6 %gather_fusion = bf16[16,4000]{1,0:T(8,128)(2,1)S(1)} fusion(bf16[400,4000]{1,0:T(8,128)(2,1)S(1)} %copy-done, s32[1024]{0:T(1024)S(1)} %pad_clamp_fusion), kind=kCustom, calls=%fused_computation | custom fusion | bytes 256064 | tf_op jit(solution)/shard_map/gather | solution.py:263
  2.6 51.0 %shard_map.73 = f32[512,2048]{1,0:T(8,128)S(1)} custom-call(bf16[32,16,128]{2,1,0:T(8,128)(2,1)S(1)} %bitcast_bitcast_fusion.picked_ref, s32[8,4,16]{2,1,0:T(4,128)} %bitcast.9, s32[8,4,16]{2,1,0:T(4,128)} %bitcast.10, s32[8]{0:T(128)} %assign_hbm.1, f32[32]{0:T(128)} %metric_hbm.1, bf16[8,16,4,128,128]{4,3,2,1,0:T(8,128)(2,1)} %b_ref.1), custom_call_target="tpu_custom_call" | custom-call | tf_op jit(solution)/shard_map/pallas_call | solution.py:274
  53.6 2.0 %copy.12 = f32[512,2048]{1,0:T(8,128)} copy(f32[512,2048]{1,0:T(8,128)S(1)} %shard_map.73) | data formatting | bytes 8388608
  (1 shorter events, 0.0 us)
Async XLA Ops:
  0.0 1.9 %copy-start = (bf16[400,4000]{1,0:T(8,128)(2,1)S(1)}, bf16[400,4000]{1,0:T(8,128)(2,1)}, u32[]{:S(2)}) copy-start(bf16[400,4000]{1,0:T(8,128)(2,1)} %param.12) | copy-start | bytes 9600004

commit v5 on v4

--- a/solution.py
+++ b/solution.py
@@ -9,7 +9,7 @@
 MESH = pl.DeviceIdType.MESH
 HALVES = 2
 COL_TILE = 512
-PIECES = 2
+PIECES = 1
 VMEM_GRANT = 44 << 20
 
 

time: 55.8 us -> 53 us (0.950)
  Pallas kernels: 51 us -> 48.1 us
    pallas_call x1, Pallas kernels: 51 us -> 48.1 us  [per_device(): pl.pallas_call(functools.partial(kernel, (nz, nx, n_basis)), out_shape=ja...]
where the time goes in v5:
time: 53 us; the launch traced here: 52.8 us
  Pallas kernels  48.1 us (91%)
  local copies, waits for them, and re-layouts  3.8 us (7%)
  other arithmetic  0.81 us (2%)
    pallas_call x1, Pallas kernels, per_device(): pl.pallas_call(functools.partial(kernel, (nz, nx, n_basis)), out_shape=ja...  48.1 us
    unnamed x3, local copies, waits for them, and re-layouts  3.15 us

profile of v5, /device:TPU:0, one launch (start us, length us, event | category | flops | bytes accessed | tf_op | source)
XLA Modules:
  0.0 52.8 jit_solution(735924942311365096)
XLA Ops:
  0.0 0.0 copy-start
  0.0 0.8 %pad_clamp_fusion = s32[1024]{0:T(1024)S(1)} fusion(s32[16]{0:T(128)} %param.13), kind=kLoop, calls=%fused_computation.3 | loop fusion | flops 1024 | bytes 4160 | tf_op jit(solution)/shard_map/gather | solution.py:263
  0.8 1.1 %copy-done = bf16[400,4000]{1,0:T(8,128)(2,1)S(1)} copy-done((bf16[400,4000]{1,0:T(8,128)(2,1)S(1)}, bf16[400,4000]{1,0:T(8,128)(2,1)}, u32[]{:S(2)}) %copy-start) | copy-done | bytes 3200024
  1.9 0.6 %gather_fusion = bf16[16,4000]{1,0:T(8,128)(2,1)S(1)} fusion(bf16[400,4000]{1,0:T(8,128)(2,1)S(1)} %copy-done, s32[1024]{0:T(1024)S(1)} %pad_clamp_fusion), kind=kCustom, calls=%fused_computation | custom fusion | bytes 256064 | tf_op jit(solution)/shard_map/gather | solution.py:263
  2.6 48.1 %shard_map.73 = f32[512,2048]{1,0:T(8,128)S(1)} custom-call(bf16[32,16,128]{2,1,0:T(8,128)(2,1)S(1)} %bitcast_bitcast_fusion.picked_ref, s32[8,4,16]{2,1,0:T(4,128)} %bitcast.9, s32[8,4,16]{2,1,0:T(4,128)} %bitcast.10, s32[8]{0:T(128)} %assign_hbm.1, f32[32]{0:T(128)} %metric_hbm.1, bf16[8,16,4,128,128]{4,3,2,1,0:T(8,128)(2,1)} %b_ref.1), custom_call_target="tpu_custom_call" | custom-call | tf_op jit(solution)/shard_map/pallas_call | solution.py:274
  50.8 2.0 %copy.12 = f32[512,2048]{1,0:T(8,128)} copy(f32[512,2048]{1,0:T(8,128)S(1)} %shard_map.73) | data formatting | bytes 8388608
  (1 shorter events, 0.0 us)
Async XLA Ops:
  0.0 1.9 %copy-start = (bf16[400,4000]{1,0:T(8,128)(2,1)S(1)}, bf16[400,4000]{1,0:T(8,128)(2,1)}, u32[]{:S(2)}) copy-start(bf16[400,4000]{1,0:T(8,128)(2,1)} %param.12) | copy-start | bytes 9600004

commit v6 on v5

--- a/solution.py
+++ b/solution.py
@@ -222,10 +222,12 @@
 
     def advance(k, carry):
         relay(k)
-        accumulate(k)
+        accumulate(k + HALVES - 1)
         return carry
 
-    lax.fori_loop(0, events + HALVES, advance, 0)
+    for h in range(HALVES - 1):
+        accumulate(h)
+    lax.fori_loop(0, events + 1, advance, 0)
 
     def drain(i, carry):
         origin = i // (np_dev * PIECES)

time: 53 us -> 52.9 us (level); the launches traced: 52.8 us -> 52.1 us
  Pallas kernels: 48.1 us -> 47.4 us
    pallas_call x1, Pallas kernels: 48.1 us -> 47.4 us  [per_device(): pl.pallas_call(functools.partial(kernel, (nz, nx, n_basis)), out_shape=ja...]
where the time goes in v6:
time: 52.9 us; the launch traced here: 52.1 us
  Pallas kernels  47.4 us (90%)
  local copies, waits for them, and re-layouts  3.8 us (7%)
  other arithmetic  0.81 us (2%)
    pallas_call x1, Pallas kernels, per_device(): pl.pallas_call(functools.partial(kernel, (nz, nx, n_basis)), out_shape=ja...  47.4 us
    unnamed x3, local copies, waits for them, and re-layouts  3.15 us

profile of v6, /device:TPU:0, one launch (start us, length us, event | category | flops | bytes accessed | tf_op | source)
XLA Modules:
  0.0 52.1 jit_solution(8203558496279831872)
XLA Ops:
  0.0 0.0 copy-start
  0.0 0.8 %pad_clamp_fusion = s32[1024]{0:T(1024)S(1)} fusion(s32[16]{0:T(128)} %param.13), kind=kLoop, calls=%fused_computation.3 | loop fusion | flops 1024 | bytes 4160 | tf_op jit(solution)/shard_map/gather | solution.py:265
  0.8 1.1 %copy-done = bf16[400,4000]{1,0:T(8,128)(2,1)S(1)} copy-done((bf16[400,4000]{1,0:T(8,128)(2,1)S(1)}, bf16[400,4000]{1,0:T(8,128)(2,1)}, u32[]{:S(2)}) %copy-start) | copy-done | bytes 3200024
  1.9 0.6 %gather_fusion = bf16[16,4000]{1,0:T(8,128)(2,1)S(1)} fusion(bf16[400,4000]{1,0:T(8,128)(2,1)S(1)} %copy-done, s32[1024]{0:T(1024)S(1)} %pad_clamp_fusion), kind=kCustom, calls=%fused_computation | custom fusion | bytes 256064 | tf_op jit(solution)/shard_map/gather | solution.py:265
  2.6 47.4 %shard_map.73 = f32[512,2048]{1,0:T(8,128)S(1)} custom-call(bf16[32,16,128]{2,1,0:T(8,128)(2,1)S(1)} %bitcast_bitcast_fusion.picked_ref, s32[8,4,16]{2,1,0:T(4,128)} %bitcast.9, s32[8,4,16]{2,1,0:T(4,128)} %bitcast.10, s32[8]{0:T(128)} %assign_hbm.1, f32[32]{0:T(128)} %metric_hbm.1, bf16[8,16,4,128,128]{4,3,2,1,0:T(8,128)(2,1)} %b_ref.1), custom_call_target="tpu_custom_call" | custom-call | tf_op jit(solution)/shard_map/pallas_call | solution.py:276
  50.0 2.0 %copy.12 = f32[512,2048]{1,0:T(8,128)} copy(f32[512,2048]{1,0:T(8,128)S(1)} %shard_map.73) | data formatting | bytes 8388608
  (1 shorter events, 0.0 us)
Async XLA Ops:
  0.0 1.9 %copy-start = (bf16[400,4000]{1,0:T(8,128)(2,1)S(1)}, bf16[400,4000]{1,0:T(8,128)(2,1)}, u32[]{:S(2)}) copy-start(bf16[400,4000]{1,0:T(8,128)(2,1)} %param.12) | copy-start | bytes 9600004
